TPU v7x, 32 devices: a whole 2x2x4 slice. The times are simulated.
32 devices in a mesh: chan: 4 (over y, core), seq: 8 (over z, x).
Axes of the slice: x: 2, y: 2, z: 4, core: 2. Of those that a mesh axis runs over, the one named last changes fastest.
Arguments:
- query_proj: bfloat16 [65536, 2048], P('seq', 'chan'), may hold values from -6 to 6
- key_proj: bfloat16 [65536, 2048], P('seq', 'chan'), may hold values from -6 to 6
- value_proj: bfloat16 [65536, 2048], P('seq', 'chan'), may hold values from -6 to 6
- short_taps: float32 [3, 3, 2048], P(None, None, 'chan'), may hold values from -3.5 to 3.5
- skip_gain: float32 [2048], P('chan'), may hold values from -6 to 6
- long_filter: float32 [4, 65536], P('chan', 'seq'), may hold values from -0.0234375 to 0.0234375
Outputs:
- mixed: float32 [65536, 2048], P('seq', 'chan')
All inputs are finite; a program needn't handle non-finite values.
Results may differ from a plain program's by a relative error of at most 0.0003.
Values may be sent and summed in bfloat16 or wider, within the bound.
No kernel may reach another device: no remote copies, remote signals or barrier semaphores. Data moves between devices by JAX's collectives and lax.ppermute only.
A program may use at most 256 MiB of HBM per device.

v0:
```python
from functools import partial
import math
import jax
import jax.numpy as jnp
from jax import lax
from jax.sharding import PartitionSpec as P

A = 256
B = 256
EXACT = lax.Precision.HIGHEST


def from_behind(value, axis, steps):
    count = lax.axis_size(axis)
    initial, last = (max(0, -steps), min(count, count - steps))
    return lax.ppermute(value, axis, [(source, source + steps) for source in range(initial, last)])


def phase_table(count_rows, count_cols, period, col_start):
    row_index = lax.broadcasted_iota(jnp.int32, (count_rows, count_cols), 0)
    col_index = lax.broadcasted_iota(jnp.int32, (count_rows, count_cols), 1) + col_start
    residue = row_index * col_index % period
    angle_val = 2.0 * math.pi / period * residue.astype(jnp.float32)
    return (jnp.cos(angle_val), jnp.sin(angle_val))


def complex_apply(pattern, matrix_re, matrix_im, data_re, data_im):
    product = partial(jnp.einsum, pattern, precision=EXACT)
    if data_im is None:
        return (product(matrix_re, data_re), product(matrix_im, data_re))
    return (
        product(matrix_re, data_re) - product(matrix_im, data_im),
        product(matrix_re, data_im) + product(matrix_im, data_re),
    )


def complex_times(first_re, first_im, second_re, second_im):
    return (
        first_re * second_re - first_im * second_im,
        first_re * second_im + first_im * second_re,
    )


def lane_forward(block, twiddle_re, twiddle_im):
    cos_b, sin_b = phase_table(B, B, B, 0)
    inner_re, inner_im = complex_apply("kb,bam->kam", cos_b, -sin_b, block[:, :, 0], block[:, :, 1])
    return complex_times(inner_re, inner_im, twiddle_re[:, :, None], -twiddle_im[:, :, None])


def lane_spectrum(block):
    cos_a, sin_a = phase_table(A, A, A, 0)
    return complex_apply("ja,kam->kjm", cos_a, -sin_a, block[:, :, 0], block[:, :, 1])


def lane_unspectrum(spec_re, spec_im):
    cos_a, sin_a = phase_table(A, A, A, 0)
    return complex_apply("ja,kjm->kam", cos_a, sin_a, spec_re, spec_im)


def lane_backward(block, twiddle_re, twiddle_im):
    turned_re, turned_im = complex_times(
        block[:, :, 0], block[:, :, 1], twiddle_re[:, :, None], twiddle_im[:, :, None]
    )
    cos_b, sin_b = phase_table(B, B, B, 0)
    out_re, out_im = complex_apply("kb,kam->bam", cos_b, sin_b, turned_re, turned_im)
    factor = 1.0 / (A * B)
    return (out_re * factor, out_im * factor)


def per_device(query_proj, key_proj, value_proj, short_taps, skip_gain, long_filter):
    tok_count, chan_width = query_proj.shape
    previous = from_behind((query_proj[-2:], key_proj[-2:], value_proj[-2:]), "seq", 1)

    def depthwise(signal, before, column):
        padded = jnp.concatenate([before, signal], axis=0).astype(jnp.float32)
        return (
            short_taps[0, column] * padded[2:]
            + short_taps[1, column] * padded[1:-1]
            + short_taps[2, column] * padded[:-2]
        )

    query_short = depthwise(query_proj, previous[0], 0)
    key_short = depthwise(key_proj, previous[1], 1)
    value_short = depthwise(value_proj, previous[2], 2)
    gated = key_short * value_short
    seq_count = lax.axis_size("seq")
    low_count = A // seq_count
    high_count = tok_count // A
    half_width = chan_width // 2
    signal_block = gated.reshape(high_count, A, 2, half_width)
    filter_taps_local = long_filter.reshape(high_count, A, 1, 1)
    filter_block = jnp.concatenate([filter_taps_local, jnp.zeros_like(filter_taps_local)], axis=2)
    signal_block, filter_block = (
        lax.all_to_all(signal_block, "seq", split_axis=1, concat_axis=0, tiled=True),
        lax.all_to_all(filter_block, "seq", split_axis=1, concat_axis=0, tiled=True),
    )
    position = lax.axis_index("seq")
    twiddle_re, twiddle_im = phase_table(B, low_count, A * B, position * low_count)
    sig_re, sig_im = lane_forward(signal_block, twiddle_re, twiddle_im)
    fil_re, fil_im = lane_forward(filter_block, twiddle_re, twiddle_im)
    signal_block, filter_block = (
        lax.all_to_all(
            jnp.stack([sig_re, sig_im], axis=2), "seq", split_axis=0, concat_axis=1, tiled=True
        ),
        lax.all_to_all(
            jnp.stack([fil_re, fil_im], axis=2), "seq", split_axis=0, concat_axis=1, tiled=True
        ),
    )
    freq_re, freq_im = lane_spectrum(signal_block)
    spectrum_re, spectrum_im = lane_spectrum(filter_block)
    mult_re, mult_im = complex_times(freq_re, freq_im, spectrum_re, spectrum_im)
    back_re, back_im = lane_unspectrum(mult_re, mult_im)
    back_block = lax.all_to_all(
        jnp.stack([back_re, back_im], axis=2), "seq", split_axis=1, concat_axis=0, tiled=True
    )
    conv_re, conv_im = lane_backward(back_block, twiddle_re, twiddle_im)
    convolved = lax.all_to_all(
        jnp.stack([conv_re, conv_im], axis=2), "seq", split_axis=0, concat_axis=1, tiled=True
    )
    convolved = convolved.reshape(tok_count, chan_width)
    return query_short * (convolved + skip_gain * gated)


def solution(mesh):
    return jax.shard_map(
        per_device,
        mesh=mesh,
        in_specs=(
            P("seq", "chan"),
            P("seq", "chan"),
            P("seq", "chan"),
            P(None, None, "chan"),
            P("chan"),
            P("chan", "seq"),
        ),
        out_specs=P("seq", "chan"),
        check_vma=False,
    )
```

profile of v0, /device:TPU:20, one launch (start us, length us, event | category | flops | bytes accessed | tf_op | source)
XLA Modules:
  0.0 2002.1 jit_solution(7467788233628211995)
XLA Ops:
  33.5 39.5 %fusion.1 = f32[8192,512]{1,0:T(8,128)} fusion(f32[8194,512]{1,0:T(8,128)} %maximum_convert_fusion.2, f32[8194,512]{1,0:T(8,128)} %maximum_convert_fusion.1, f32[512]{0:T(512)S(1)} %bitcast.234, f32[512]{0:T(512)S(1)} %bitcast.235, f32[512]{0:T(512)S(1)} %bitcast.230, f32[512]{0:T(512)S(1)} %bitcast.231, f32[512]{0:T(512)S(1)} %bitcast.232, f32[512]{0:T(512)S(1)} %bitcast.233), kind=kLoop, calls=%fused_computation.2 | loop fusion | flops 46137344 | bytes 117452800 | tf_op jit(solution)/shard_map/mul | solution.py:85
  73.0 19.9 reshape.143
  92.9 17.7 copy.125
  127.1 348.4 %all-to-all-done = f32[32,256,2,256]{3,0,2,1:T(8,128)} async-done(((f32[32,256,2,256]{3,0,2,1:T(8,128)}), f32[32,256,2,256]{3,0,2,1:T(8,128)}, u32[]{:S(2)}, u32[]{:S(2)}) %all-to-all-start) | async-done | bytes 16777248 | tf_op jit(solution)/shard_map/all_to_all | solution.py:94
  489.5 11.7 fusion.16
  512.8 11.8 fusion.19
  524.7 21.5 %subtract_bitcast_fusion.1 = (f32[256,32,1,256]{3,0,1,2:T(8,128)}, f32[256,32,1,256]{3,0,1,2:T(8,128)}) fusion(f32[256,32]{0,1:T(8,128)S(1)} %get-tuple-element.21, f32[256,32]{0,1:T(8,128)S(1)} %get-tuple-element.24, f32[256,32,256]{2,0,1:T(8,128)} %fusion.16, f32[256,32,256]{2,0,1:T(8,128)} %fusion.17, f32[256,32,256]{2,0,1:T(8,128)} %fusion.19, ...), kind=kOutput, calls=%fused_computation.46 | convolution fusion | flops 6460145664 | bytes 50397184 | tf_op jit(solution)/shard_map/kb,bam->kam/dot_general | solution.py:33
  553.1 20.2 %copy.132 = f32[256,32,2,256]{3,1,2,0:T(8,128)} copy(f32[256,32,2,256]{3,0,1,2:T(8,128)S(1)} %pad_maximum_fusion) | data formatting | bytes 33554432 | tf_op jit(solution)/shard_map/stack | solution.py:103
  585.8 352.9 %all-to-all-done.1 = f32[256,32,2,256]{3,1,2,0:T(8,128)} async-done(((f32[256,32,2,256]{3,1,2,0:T(8,128)}), f32[256,32,2,256]{3,1,2,0:T(8,128)}, u32[]{:S(2)}, u32[]{:S(2)}) %all-to-all-start.1) | async-done | bytes 16777248 | tf_op jit(solution)/shard_map/all_to_all | solution.py:102
  945.3 18.3 fusion.20
  963.6 18.0 fusion.21
  981.6 18.1 fusion.23
  999.7 25.9 %multiply_subtract_fusion.1 = (f32[32,256,256]{2,1,0:T(8,128)}, f32[32,256,256]{2,1,0:T(8,128)}) fusion(f32[32,256]{1,0:T(8,128)S(1)} %convolution_add_fusion, f32[32,256]{1,0:T(8,128)S(1)} %convolution_subtract_fusion, f32[32,256,256]{2,1,0:T(8,128)} %fusion.20, f32[32,256,256]{2,1,0:T(8,128)} %fusion.21, f32[32,256,256]{2,1,0:T(8,128)} %fusion.23, ...), kind=kOutput, calls=%fused_computation.44 | convolution fusion | flops 6460145664 | bytes 50397184 | tf_op jit(solution)/shard_map/ja,kam->kjm/dot_general | solution.py:33
  1025.7 13.4 fusion.10
  1078.7 19.9 copy.149
  1098.6 368.1 %all_to_all.105 = f32[32,256,2,256]{3,0,2,1:T(8,128)S(1)} all-to-all(f32[32,256,2,256]{3,0,2,1:T(8,128)} %copy.149), channel_id=1, replica_groups=mesh['chan'=4,'seq'=8] {'seq'}, dimensions={1} | all-to-all | bytes 33554432 | tf_op jit(solution)/shard_map/all_to_all | solution.py:113
  1468.8 12.5 fusion.28
  1481.2 12.6 fusion.29
  1493.9 17.5 multiply_bitcast_fusion.1
  1511.4 16.1 multiply_bitcast_fusion
  1534.3 20.3 %copy.152 = f32[256,32,2,256]{3,1,2,0:T(8,128)} copy(f32[256,32,2,256]{3,0,1,2:T(8,128)S(1)} %pad_maximum_fusion.2) | data formatting | bytes 33554432 | tf_op jit(solution)/shard_map/stack | solution.py:118
  1566.9 356.4 %collective-permute-done = bf16[2,512]{1,0:T(2,128)(2,1)S(1)} collective-permute-done((bf16[2,512]{1,0:T(2,128)(2,1)S(1)}, bf16[2,512]{1,0:T(2,128)(2,1)S(1)}, u32[]{:S(2)}, u32[]{:S(2)}) %collective-permute-start) | collective-permute-done | bytes 2080 | tf_op jit(solution)/shard_map/ppermute | solution.py:16
  1933.1 27.6 %copy.153 = f32[32,8,32,2,256]{4,3,2,1,0:T(2,128)S(1)} copy(f32[32,8,32,2,256]{4,2,3,0,1:T(8,128)} %bitcast.62) | data formatting | bytes 33554432 | tf_op jit(solution)/shard_map/all_to_all | solution.py:117
  1968.0 33.7 %fusion.6 = f32[8192,512]{1,0:T(8,128)} fusion(f32[8194,512]{1,0:T(8,128)} %maximum_convert_fusion, f32[8192,512]{1,0:T(8,128)} %bitcast.215, f32[8192,512]{1,0:T(8,128)} %fusion.1, f32[512]{0:T(512)S(1)} %copy-done.9, f32[512]{0:T(512)S(1)} %bitcast.228, f32[512]{0:T(512)S(1)} %bitcast.229, f32[512]{0:T(512)S(1)} %bitcast.227), kind=kLoop, calls=%fused_computation.13 | loop fusion | flops 33554432 | bytes 100671488 | tf_op jit(solution)/shard_map/mul | solution.py:121
  (87 shorter events, 179.2 us)
Async XLA Ops:
  0.7 16.1 collective-permute-start.1
  4.8 22.4 %collective-permute-start.2 = (bf16[2,512]{1,0:T(2,128)(2,1)S(1)}, bf16[2,512]{1,0:T(2,128)(2,1)S(1)}, u32[]{:S(2)}, u32[]{:S(2)}) collective-permute-start(bf16[2,512]{1,0:T(2,128)(2,1)S(1)} %slice.108), channel_id=1, source_target_pairs={{0,1},{1,2},{2,3},{3,4},{4,5},{5,6},{6,7},{8,9},{9,10},{10,11},{11... | collective-permute-start | bytes 6152 | tf_op jit(solution)/shard_map/ppermute | solution.py:16
  10.1 100.4 %all-to-all-start.2 = ((f32[8,1,2048]{2,1,0:T(1,128)}), f32[8,1,2048]{2,1,0:T(1,128)S(1)}, u32[]{:S(2)}, u32[]{:S(2)}) async-start(f32[8,1,2048]{2,1,0:T(1,128)} %reshape.153), calls=%async_computation.2 | async-start | bytes 131072 | tf_op jit(solution)/shard_map/all_to_all | solution.py:95
  15.3 11.9 slice-start.2
  16.8 10.4 slice-start.3
  110.6 364.9 %all-to-all-start = ((f32[32,256,2,256]{3,0,2,1:T(8,128)}), f32[32,256,2,256]{3,0,2,1:T(8,128)}, u32[]{:S(2)}, u32[]{:S(2)}) async-start(f32[32,256,2,256]{3,0,2,1:T(8,128)} %copy.125), calls=%async_computation | async-start | bytes 33554432 | tf_op jit(solution)/shard_map/all_to_all | solution.py:94
  475.5 97.8 %all-to-all-start.3 = ((f32[8,1,2048]{2,1,0:T(1,128)}), f32[8,1,2048]{2,1,0:T(1,128)S(1)}, u32[]{:S(2)}, u32[]{:S(2)}) async-start(f32[8,1,2048]{2,1,0:T(1,128)} %reshape.155), calls=%async_computation.3 | async-start | bytes 131072 | tf_op jit(solution)/shard_map/all_to_all | solution.py:105
  489.5 23.3 %copy-start.2 = (f32[8,32,32,2,256]{4,1,0,2,3:T(8,128)}, f32[8,32,32,2,256]{4,1,0,2,3:T(8,128)S(1)}, u32[]{:S(2)}) copy-start(f32[8,32,32,2,256]{4,1,0,2,3:T(8,128)S(1)} %copy.127) | copy-start | bytes 50331652
  573.3 365.4 %all-to-all-start.1 = ((f32[256,32,2,256]{3,1,2,0:T(8,128)}), f32[256,32,2,256]{3,1,2,0:T(8,128)}, u32[]{:S(2)}, u32[]{:S(2)}) async-start(f32[256,32,2,256]{3,1,2,0:T(8,128)} %copy.132), calls=%async_computation.1 | async-start | bytes 33554432 | tf_op jit(solution)/shard_map/all_to_all | solution.py:102
  945.3 36.3 %copy-start.1 = (f32[32,8,32,2,256]{4,2,1,3,0:T(8,128)}, f32[32,8,32,2,256]{4,2,1,3,0:T(8,128)S(1)}, u32[]{:S(2)}) copy-start(f32[32,8,32,2,256]{4,2,1,3,0:T(8,128)S(1)} %copy.133) | copy-start | bytes 50331652
  1025.7 13.4 copy-start.3
  1025.7 21.1 %slice-start = ((s8[8388608]{0:T(1024)(128)(4,1)}), s8[4194304]{0:T(1024)(128)(4,1)S(1)}, s32[]{:S(2)}) async-start(s8[8388608]{0:T(1024)(128)(4,1)} %bitcast.213), calls=%async_computation.6 | async-start | bytes 8388608
  1039.1 7.7 slice-start.1
  1466.7 2.1 copy-start.5
  1468.7 12.5 copy-start
  1493.9 17.5 copy-start.4
  1554.7 378.4 %all-to-all-start.5 = ((f32[256,32,2,256]{3,1,2,0:T(8,128)}), f32[256,32,2,256]{3,1,2,0:T(8,128)}, u32[]{:S(2)}, u32[]{:S(2)}) async-start(f32[256,32,2,256]{3,1,2,0:T(8,128)} %copy.152), calls=%async_computation.5 | async-start | bytes 33554432 | tf_op jit(solution)/shard_map/all_to_all | solution.py:117
  1563.5 359.7 %collective-permute-start = (bf16[2,512]{1,0:T(2,128)(2,1)S(1)}, bf16[2,512]{1,0:T(2,128)(2,1)S(1)}, u32[]{:S(2)}, u32[]{:S(2)}) collective-permute-start(bf16[2,512]{1,0:T(2,128)(2,1)S(1)} %slice.94), channel_id=1, source_target_pairs={{0,1},{1,2},{2,3},{3,4},{4,5},{5,6},{6,7},{8,9},{9,10},{10,11},{11... | collective-permute-start | bytes 6152 | tf_op jit(solution)/shard_map/ppermute | solution.py:16
  1960.7 7.3 copy-start.6
  1960.7 7.3 copy-start.7
  1960.7 7.3 copy-start.8
  1960.7 7.3 copy-start.9
where the time goes:
time: 2010 us; the launch traced here: 2000 us
  waiting for transfers between devices  1060 us (53%)
  blocking collectives  368 us (18%)
  matrix products  249 us (12%)
  local copies, waits for them, and re-layouts  157 us (8%)
  other arithmetic  126 us (6%)
  starting transfers between devices  43.1 us (2%)
    all_to_all x1, blocking collectives, per_device(): lax.all_to_all(jnp.stack([back_re, back_im], axis=2), 'seq', split_axis=1...  368 us
    ppermute x3, waiting for transfers between devices, from_behind(): lax.ppermute(value, axis, [(source, source + steps) for source in range(i...  356 us
    all_to_all x1, waiting for transfers between devices, per_device(): lax.all_to_all(jnp.stack([sig_re, sig_im], axis=2), 'seq', split_axis=0,...  353 us
    all_to_all x1, waiting for transfers between devices, per_device(): lax.all_to_all(signal_block, 'seq', split_axis=1, concat_axis=0, tiled=True)  348 us
    dot_general x6, matrix products, complex_apply(): product(matrix_re, data_im) + product(matrix_im, data_re)  70.2 us
    dot_general x6, matrix products, complex_apply(): product(matrix_im, data_im)  64 us
    dot_general x6, matrix products, complex_apply(): product(matrix_im, data_re)  59.5 us
    dot_general x6, matrix products, complex_apply(): product(matrix_re, data_re) - product(matrix_im, data_im)  55.7 us
  transfers between devices with their start and end apart: 8, of which 3 were waited for; matrix products, arithmetic and copies ran while one was open for 11% of the time, Pallas kernels for 0%

commit v1 on v0

--- a/solution.py
+++ b/solution.py
@@ -1,3 +1,4 @@
+import functools
 from functools import partial
 import math
 import jax
@@ -8,6 +9,39 @@
 A = 256
 B = 256
 EXACT = lax.Precision.HIGHEST
+
+
+def define_indices(content, dim_i, u_in):
+    parts_out = content.shape
+    wide_out = content.reshape(
+        *parts_out[:dim_i], u_in, parts_out[dim_i] // u_in, *parts_out[dim_i + 1 :]
+    )
+    return jnp.moveaxis(wide_out, dim_i, 0)
+
+
+def _read_skins(body, at_axis):
+    body = jnp.moveaxis(body, 0, at_axis)
+    taken_in = body.shape
+    return body.reshape(
+        *taken_in[:at_axis], taken_in[at_axis] * taken_in[at_axis + 1], *taken_in[at_axis + 2 :]
+    )
+
+
+def ends_order(obj, chip_axis, payload, array_in):
+    big, block_out = (jax.lax.psum(1, chip_axis), jax.lax.axis_index(chip_axis))
+    main = define_indices(obj, payload, big)
+    now = main
+    for it in range(1, big):
+        aux, tile_out = ((block_out + it) % big, (block_out - it) % big)
+        side_arr = lax.dynamic_index_in_dim(main, aux, 0)
+        carry_in = jax.lax.ppermute(
+            side_arr, chip_axis, [(dev_i, (dev_i + it) % big) for dev_i in range(big)]
+        )
+        now = lax.dynamic_update_slice_in_dim(now, carry_in, tile_out, axis=0)
+    return _read_skins(now, array_in)
+
+
+point_space_now = functools.partial(ends_order, chip_axis="seq", payload=0, array_in=1)
 
 
 def from_behind(value, axis, steps):
@@ -99,9 +133,7 @@
     sig_re, sig_im = lane_forward(signal_block, twiddle_re, twiddle_im)
     fil_re, fil_im = lane_forward(filter_block, twiddle_re, twiddle_im)
     signal_block, filter_block = (
-        lax.all_to_all(
-            jnp.stack([sig_re, sig_im], axis=2), "seq", split_axis=0, concat_axis=1, tiled=True
-        ),
+        point_space_now(jnp.stack([sig_re, sig_im], axis=2)),
         lax.all_to_all(
             jnp.stack([fil_re, fil_im], axis=2), "seq", split_axis=0, concat_axis=1, tiled=True
         ),

time: 2010 us -> 2080 us (1.035)
  starting transfers between devices: 43.1 us -> 228 us
  waiting for transfers between devices: 1060 us -> 919 us
  local copies, waits for them, and re-layouts: 157 us -> 182 us
    all_to_all x1 -> x0, waiting for transfers between devices: 353 us -> none  [per_device(): lax.all_to_all(jnp.stack([sig_re, sig_im], axis=2), 'seq', split_axis=0,...]
    ppermute x0 -> x7, starting transfers between devices: none -> 192 us  [ends_order(): jax.lax.ppermute(side_arr, chip_axis, [(dev_i, (dev_i + it) % big) for de...]
    all_to_all x1, waiting for transfers between devices: 0.01 us -> 126 us  [per_device(): lax.all_to_all(jnp.stack([fil_re, fil_im], axis=2), 'seq', split_axis=0,...]
    ppermute x0 -> x7, waiting for transfers between devices: none -> 85.8 us  [ends_order(): jax.lax.ppermute(side_arr, chip_axis, [(dev_i, (dev_i + it) % big) for de...]
  transfers between devices with their start and end apart: 8 -> 14, of which waited for: 3 -> 5; matrix products, arithmetic and copies ran while one was open for 11% -> 7% of each run, Pallas kernels for 0% -> 0%
where the time goes in v1:
time: 2080 us; the launch traced here: 2070 us
  waiting for transfers between devices  919 us (44%)
  blocking collectives  369 us (18%)
  matrix products  252 us (12%)
  starting transfers between devices  228 us (11%)
  local copies, waits for them, and re-layouts  182 us (9%)
  other arithmetic  119 us (6%)
    all_to_all x1, blocking collectives, per_device(): lax.all_to_all(jnp.stack([back_re, back_im], axis=2), 'seq', split_axis=1...  369 us
    ppermute x3, waiting for transfers between devices, from_behind(): lax.ppermute(value, axis, [(source, source + steps) for source in range(i...  356 us
    all_to_all x1, waiting for transfers between devices, per_device(): lax.all_to_all(signal_block, 'seq', split_axis=1, concat_axis=0, tiled=True)  351 us
    ppermute x7, starting transfers between devices, ends_order(): jax.lax.ppermute(side_arr, chip_axis, [(dev_i, (dev_i + it) % big) for de...  192 us
    all_to_all x1, waiting for transfers between devices, per_device(): lax.all_to_all(jnp.stack([fil_re, fil_im], axis=2), 'seq', split_axis=0,...  126 us
    ppermute x7, waiting for transfers between devices, ends_order(): jax.lax.ppermute(side_arr, chip_axis, [(dev_i, (dev_i + it) % big) for de...  85.8 us
    dot_general x6, matrix products, complex_apply(): product(matrix_re, data_im) + product(matrix_im, data_re)  70.4 us
    dot_general x6, matrix products, complex_apply(): product(matrix_im, data_im)  64.3 us
  transfers between devices with their start and end apart: 14, of which 5 were waited for; matrix products, arithmetic and copies ran while one was open for 7% of the time, Pallas kernels for 0%

profile of v1, /device:TPU:20, one launch (start us, length us, event | category | flops | bytes accessed | tf_op | source)
XLA Modules:
  0.0 2069.3 jit_solution(17651047371941265431)
XLA Ops:
  33.5 39.5 %fusion.1 = f32[8192,512]{1,0:T(8,128)} fusion(f32[8194,512]{1,0:T(8,128)} %maximum_convert_fusion.2, f32[8194,512]{1,0:T(8,128)} %maximum_convert_fusion.1, f32[512]{0:T(512)S(1)} %bitcast.233, f32[512]{0:T(512)S(1)} %bitcast.234, f32[512]{0:T(512)S(1)} %bitcast.229, f32[512]{0:T(512)S(1)} %bitcast.230, f32[512]{0:T(512)S(1)} %bitcast.231, f32[512]{0:T(512)S(1)} %bitcast.232), kind=kLoop, calls=%fused_computation.2 | loop fusion | flops 46137344 | bytes 117452800 | tf_op jit(solution)/shard_map/mul | solution.py:119
  73.0 19.9 reshape.152
  92.9 17.7 copy.128
  124.5 351.2 %all-to-all-done = f32[32,256,2,256]{3,0,2,1:T(8,128)} async-done(((f32[32,256,2,256]{3,0,2,1:T(8,128)}), f32[32,256,2,256]{3,0,2,1:T(8,128)}, u32[]{:S(2)}, u32[]{:S(2)}) %all-to-all-start) | async-done | bytes 16777248 | tf_op jit(solution)/shard_map/all_to_all | solution.py:128
  517.5 21.9 %multiply_add_fusion.2 = (f32[256,32,256]{2,0,1:T(8,128)}, f32[256,32,256]{2,0,1:T(8,128)}) fusion(f32[256,32]{0,1:T(8,128)S(1)} %get-tuple-element.28, f32[256,32]{0,1:T(8,128)S(1)} %get-tuple-element.31, f32[256,32,256]{2,0,1:T(8,128)} %fusion.16, f32[256,32,256]{2,0,1:T(8,128)} %fusion.17, f32[256,32,256]{2,0,1:T(8,128)} %fusion.19, ...), kind=kOutput, calls=%fused_computation.46 | convolution fusion | flops 6460145664 | bytes 50397184 | tf_op jit(solution)/shard_map/kb,bam->kam/dot_general | solution.py:67
  564.0 45.9 %collective-permute-done.3 = f32[1,32,32,2,256]{4,2,0,3,1:T(8,128)} collective-permute-done((f32[1,32,32,2,256]{4,2,0,3,1:T(8,128)S(1)}, f32[1,32,32,2,256]{4,2,0,3,1:T(8,128)}, u32[]{:S(2)}, u32[]{:S(2)}) %collective-permute-start.3) | collective-permute-done | bytes 2097184 | tf_op jit(solution)/shard_map/ppermute | solution.py:37
  631.9 39.9 %collective-permute-done.4 = f32[1,32,32,2,256]{4,2,0,3,1:T(8,128)S(1)} collective-permute-done((f32[1,32,32,2,256]{4,2,0,3,1:T(8,128)}, f32[1,32,32,2,256]{4,2,0,3,1:T(8,128)S(1)}, u32[]{:S(2)}, u32[]{:S(2)}) %collective-permute-start.4) | collective-permute-done | bytes 2097184 | tf_op jit(solution)/shard_map/ppermute | solution.py:37
  671.8 179.5 %collective-permute-start.9 = (f32[1,32,32,2,256]{4,2,0,3,1:T(8,128)S(1)}, f32[1,32,32,2,256]{4,2,0,3,1:T(8,128)}, u32[]{:S(2)}, u32[]{:S(2)}) collective-permute-start(f32[1,32,32,2,256]{4,2,0,3,1:T(8,128)S(1)} %get-tuple-element.9), channel_id=1, source_target_pairs={{0,7},{1,0},{2,1},{3,2},{4,3},{5,4},{6,5},{7,6},{8,15},{9,8},{10,9... | collective-permute-start | bytes 6291464 | tf_op jit(solution)/shard_map/ppermute | solution.py:37
  859.9 125.8 %all-to-all-done.2 = f32[8,1,2048]{2,1,0:T(1,128)S(1)} async-done(((f32[8,1,2048]{2,1,0:T(1,128)}), f32[8,1,2048]{2,1,0:T(1,128)S(1)}, u32[]{:S(2)}, u32[]{:S(2)}) %all-to-all-start.2) | async-done | bytes 65568 | tf_op jit(solution)/shard_map/all_to_all | solution.py:137
  1011.2 19.7 fusion.20
  1031.0 18.0 fusion.21
  1049.0 18.3 fusion.23
  1067.3 25.7 %multiply_subtract_fusion.1 = (f32[32,256,256]{2,1,0:T(8,128)}, f32[32,256,256]{2,1,0:T(8,128)}) fusion(f32[32,256]{1,0:T(8,128)S(1)} %convolution_add_fusion, f32[32,256]{1,0:T(8,128)S(1)} %convolution_subtract_fusion, f32[32,256,256]{2,1,0:T(8,128)} %fusion.20, f32[32,256,256]{2,1,0:T(8,128)} %fusion.21, f32[32,256,256]{2,1,0:T(8,128)} %fusion.23, ...), kind=kOutput, calls=%fused_computation.45 | convolution fusion | flops 6460145664 | bytes 50397184 | tf_op jit(solution)/shard_map/ja,kam->kjm/dot_general | solution.py:67
  1093.1 13.5 fusion.10
  1146.3 19.9 copy.152
  1166.2 368.6 %all_to_all.87 = f32[32,256,2,256]{3,0,2,1:T(8,128)S(1)} all-to-all(f32[32,256,2,256]{3,0,2,1:T(8,128)} %copy.152), channel_id=1, replica_groups=mesh['chan'=4,'seq'=8] {'seq'}, dimensions={1} | all-to-all | bytes 33554432 | tf_op jit(solution)/shard_map/all_to_all | solution.py:145
  1536.7 12.4 fusion.28
  1549.2 12.7 fusion.29
  1561.9 17.7 multiply_bitcast_fusion.1
  1579.6 16.1 multiply_bitcast_fusion
  1602.5 20.2 copy.155
  1634.3 356.4 %collective-permute-done = bf16[2,512]{1,0:T(2,128)(2,1)S(1)} collective-permute-done((bf16[2,512]{1,0:T(2,128)(2,1)S(1)}, bf16[2,512]{1,0:T(2,128)(2,1)S(1)}, u32[]{:S(2)}, u32[]{:S(2)}) %collective-permute-start) | collective-permute-done | bytes 2080 | tf_op jit(solution)/shard_map/ppermute | solution.py:50
  2000.5 27.6 %copy.156 = f32[32,8,32,2,256]{4,3,2,1,0:T(2,128)S(1)} copy(f32[32,8,32,2,256]{4,2,3,0,1:T(8,128)} %bitcast.62) | data formatting | bytes 33554432 | tf_op jit(solution)/shard_map/all_to_all | solution.py:149
  2035.4 33.7 %fusion.6 = f32[8192,512]{1,0:T(8,128)} fusion(f32[8194,512]{1,0:T(8,128)} %maximum_convert_fusion, f32[8192,512]{1,0:T(8,128)} %bitcast.212, f32[8192,512]{1,0:T(8,128)} %fusion.1, f32[512]{0:T(512)S(1)} %copy-done.11, f32[512]{0:T(512)S(1)} %bitcast.227, f32[512]{0:T(512)S(1)} %bitcast.228, f32[512]{0:T(512)S(1)} %bitcast.226), kind=kLoop, calls=%fused_computation.13 | loop fusion | flops 33554432 | bytes 100671488 | tf_op jit(solution)/shard_map/mul | solution.py:153
  (110 shorter events, 246.8 us)
Async XLA Ops:
  0.7 16.1 collective-permute-start.1
  4.8 22.4 %collective-permute-start.2 = (bf16[2,512]{1,0:T(2,128)(2,1)S(1)}, bf16[2,512]{1,0:T(2,128)(2,1)S(1)}, u32[]{:S(2)}, u32[]{:S(2)}) collective-permute-start(bf16[2,512]{1,0:T(2,128)(2,1)S(1)} %slice.108), channel_id=1, source_target_pairs={{0,1},{1,2},{2,3},{3,4},{4,5},{5,6},{6,7},{8,9},{9,10},{10,11},{11... | collective-permute-start | bytes 6152 | tf_op jit(solution)/shard_map/ppermute | solution.py:50
  10.1 100.4 %all-to-all-start.1 = ((f32[8,1,2048]{2,1,0:T(1,128)}), f32[8,1,2048]{2,1,0:T(1,128)S(1)}, u32[]{:S(2)}, u32[]{:S(2)}) async-start(f32[8,1,2048]{2,1,0:T(1,128)} %reshape.162), calls=%async_computation.1 | async-start | bytes 131072 | tf_op jit(solution)/shard_map/all_to_all | solution.py:129
  15.3 11.9 slice-start.2
  16.8 10.4 slice-start.3
  110.6 365.1 %all-to-all-start = ((f32[32,256,2,256]{3,0,2,1:T(8,128)}), f32[32,256,2,256]{3,0,2,1:T(8,128)}, u32[]{:S(2)}, u32[]{:S(2)}) async-start(f32[32,256,2,256]{3,0,2,1:T(8,128)} %copy.128), calls=%async_computation | async-start | bytes 33554432 | tf_op jit(solution)/shard_map/all_to_all | solution.py:128
  482.3 23.5 %copy-start.3 = (f32[8,32,32,2,256]{4,1,0,2,3:T(8,128)}, f32[8,32,32,2,256]{4,1,0,2,3:T(8,128)S(1)}, u32[]{:S(2)}) copy-start(f32[8,32,32,2,256]{4,1,0,2,3:T(8,128)S(1)} %copy.130) | copy-start | bytes 50331652
  562.3 47.6 %collective-permute-start.3 = (f32[1,32,32,2,256]{4,2,0,3,1:T(8,128)S(1)}, f32[1,32,32,2,256]{4,2,0,3,1:T(8,128)}, u32[]{:S(2)}, u32[]{:S(2)}) collective-permute-start(f32[1,32,32,2,256]{4,2,0,3,1:T(8,128)S(1)} %constant_dynamic-slice_fusion.6), channel_id=1, source_target_pairs={{0,1},{1,2},{2,3},{3,4},{4,5},{5,6},{6,7},{7,0},{8,9},{9,10},{10,1... | collective-permute-start | bytes 6291464 | tf_op jit(solution)/shard_map/ppermute | solution.py:37
  620.9 50.9 %collective-permute-start.4 = (f32[1,32,32,2,256]{4,2,0,3,1:T(8,128)}, f32[1,32,32,2,256]{4,2,0,3,1:T(8,128)S(1)}, u32[]{:S(2)}, u32[]{:S(2)}) collective-permute-start(f32[1,32,32,2,256]{4,2,0,3,1:T(8,128)} %get-tuple-element.14), channel_id=1, source_target_pairs={{0,2},{1,3},{2,4},{3,5},{4,6},{5,7},{6,0},{7,1},{8,10},{9,11},{10,... | collective-permute-start | bytes 6291464 | tf_op jit(solution)/shard_map/ppermute | solution.py:37
  625.4 369.9 %collective-permute-start.5 = (f32[1,32,32,2,256]{4,2,0,3,1:T(8,128)}, f32[1,32,32,2,256]{4,2,0,3,1:T(8,128)}, u32[]{:S(2)}, u32[]{:S(2)}) collective-permute-start(f32[1,32,32,2,256]{4,2,0,3,1:T(8,128)} %get-tuple-element.13), channel_id=1, source_target_pairs={{0,3},{1,4},{2,5},{3,6},{4,7},{5,0},{6,1},{7,2},{8,11},{9,12},{10,... | collective-permute-start | bytes 6291464 | tf_op jit(solution)/shard_map/ppermute | solution.py:37
  625.9 372.6 %collective-permute-start.6 = (f32[1,32,32,2,256]{4,2,0,3,1:T(8,128)}, f32[1,32,32,2,256]{4,2,0,3,1:T(8,128)}, u32[]{:S(2)}, u32[]{:S(2)}) collective-permute-start(f32[1,32,32,2,256]{4,2,0,3,1:T(8,128)} %get-tuple-element.12), channel_id=1, source_target_pairs={{0,4},{1,5},{2,6},{3,7},{4,0},{5,1},{6,2},{7,3},{8,12},{9,13},{10,... | collective-permute-start | bytes 6291464 | tf_op jit(solution)/shard_map/ppermute | solution.py:37
  626.3 375.4 %collective-permute-start.7 = (f32[1,32,32,2,256]{4,2,0,3,1:T(8,128)}, f32[1,32,32,2,256]{4,2,0,3,1:T(8,128)}, u32[]{:S(2)}, u32[]{:S(2)}) collective-permute-start(f32[1,32,32,2,256]{4,2,0,3,1:T(8,128)} %get-tuple-element.11), channel_id=1, source_target_pairs={{0,5},{1,6},{2,7},{3,0},{4,1},{5,2},{6,3},{7,4},{8,13},{9,14},{10,... | collective-permute-start | bytes 6291464 | tf_op jit(solution)/shard_map/ppermute | solution.py:37
  629.2 375.7 %collective-permute-start.8 = (f32[1,32,32,2,256]{4,2,0,3,1:T(8,128)}, f32[1,32,32,2,256]{4,2,0,3,1:T(8,128)}, u32[]{:S(2)}, u32[]{:S(2)}) collective-permute-start(f32[1,32,32,2,256]{4,2,0,3,1:T(8,128)} %get-tuple-element.10), channel_id=1, source_target_pairs={{0,6},{1,7},{2,0},{3,1},{4,2},{5,3},{6,4},{7,5},{8,14},{9,15},{10,... | collective-permute-start | bytes 6291464 | tf_op jit(solution)/shard_map/ppermute | solution.py:37
  671.8 179.6 %copy-start.6 = (f32[1,32,32,2,256]{4,2,0,3,1:T(8,128)}, f32[1,32,32,2,256]{4,2,0,3,1:T(8,128)S(1)}, u32[]{:S(2)}) copy-start(f32[1,32,32,2,256]{4,2,0,3,1:T(8,128)S(1)} %collective-permute-done.4) | copy-start | bytes 6291460
  671.8 336.3 %collective-permute-start.9 = (f32[1,32,32,2,256]{4,2,0,3,1:T(8,128)S(1)}, f32[1,32,32,2,256]{4,2,0,3,1:T(8,128)}, u32[]{:S(2)}, u32[]{:S(2)}) collective-permute-start(f32[1,32,32,2,256]{4,2,0,3,1:T(8,128)S(1)} %get-tuple-element.9), channel_id=1, source_target_pairs={{0,7},{1,0},{2,1},{3,2},{4,3},{5,4},{6,5},{7,6},{8,15},{9,8},{10,9... | collective-permute-start | bytes 6291464 | tf_op jit(solution)/shard_map/ppermute | solution.py:37
  853.8 131.8 %all-to-all-start.2 = ((f32[8,1,2048]{2,1,0:T(1,128)}), f32[8,1,2048]{2,1,0:T(1,128)S(1)}, u32[]{:S(2)}, u32[]{:S(2)}) async-start(f32[8,1,2048]{2,1,0:T(1,128)} %reshape.164), calls=%async_computation.2 | async-start | bytes 131072 | tf_op jit(solution)/shard_map/all_to_all | solution.py:137
  1011.2 19.7 copy-start.1
  1093.0 13.5 copy-start.4
  1093.1 21.1 %slice-start = ((s8[8388608]{0:T(1024)(128)(4,1)}), s8[4194304]{0:T(1024)(128)(4,1)S(1)}, s32[]{:S(2)}) async-start(s8[8388608]{0:T(1024)(128)(4,1)} %bitcast.210), calls=%async_computation.5 | async-start | bytes 8388608
  1106.5 7.7 slice-start.1
  1536.7 12.5 copy-start.2
  1561.9 17.7 copy-start.5
  1622.8 377.7 %all-to-all-start.4 = ((f32[256,32,2,256]{3,1,2,0:T(8,128)}), f32[256,32,2,256]{3,1,2,0:T(8,128)}, u32[]{:S(2)}, u32[]{:S(2)}) async-start(f32[256,32,2,256]{3,1,2,0:T(8,128)} %copy.155), calls=%async_computation.4 | async-start | bytes 33554432 | tf_op jit(solution)/shard_map/all_to_all | solution.py:149
  1631.0 359.7 %collective-permute-start = (bf16[2,512]{1,0:T(2,128)(2,1)S(1)}, bf16[2,512]{1,0:T(2,128)(2,1)S(1)}, u32[]{:S(2)}, u32[]{:S(2)}) collective-permute-start(bf16[2,512]{1,0:T(2,128)(2,1)S(1)} %slice.94), channel_id=1, source_target_pairs={{0,1},{1,2},{2,3},{3,4},{4,5},{5,6},{6,7},{8,9},{9,10},{10,11},{11... | collective-permute-start | bytes 6152 | tf_op jit(solution)/shard_map/ppermute | solution.py:50
  (6 other events, 36.7 us)
